TPU v7x, 512 devices: a whole 4x4x16 slice. The times are simulated.
512 devices in a mesh: kgrp: 16 (over y, x), energy: 32 (over z, core).
Axes of the slice: x: 4, y: 4, z: 16, core: 2. Of those that a mesh axis runs over, the one named last changes fastest.
Arguments:
- greens: float32 [2, 2, 2, 1024, 4096], P(None, None, None, 'kgrp', 'energy'), may hold values from -6 to 6
- current: float32 [2, 2, 2, 1024, 4096], P(None, None, None, ('kgrp', 'energy')), may hold values from -6 to 6
- past_inputs: float32 [5, 2, 2, 2, 1024, 4096], P(None, None, None, None, ('kgrp', 'energy')), may hold values from -6 to 6
- past_residuals: float32 [5, 2, 2, 2, 1024, 4096], P(None, None, None, None, ('kgrp', 'energy')), may hold values from -40 to 40
- slot_order: int32 [5], replicated, may hold values from 0 to 4, each once
- neighbour: int32 [1024, 5], P('kgrp'), may hold values from 0 to 1023, as said below
- momentum_class: int32 [1024], P('kgrp'), may hold values from 0 to 3
- stencil_weight: float32 [5], replicated, may hold values from 0.1 to 0.4
- acoustic_coupling: float32 [4], replicated, may hold values from 0.3 to 1.5
- optical_coupling: float32 [2], replicated, may hold values from 0.2 to 0.6
- occupation: float32 [2], replicated, may hold values from 0.1 to 1
- phonon_shift: int32 [2], replicated, may hold values from 32 to 96, as said below
Outputs:
- mixed: float32 [2, 2, 2, 1024, 4096], P(None, None, None, ('kgrp', 'energy'))
Inputs may be any that keep to these rules, and one draw needn't show every extreme that they name: `neighbour`: each index names a momentum of the row's own group of 64 consecutive momenta or of the group just before or after it, counted periodically over all groups. `phonon_shift`: the larger of the two shifts is exactly 96.
All inputs are finite; a program needn't handle non-finite values.
Results may differ from a plain program's by a relative error of at most 0.000053.
Values sent between devices are 32-bit elements; how exact they have to be, the bound alone decides.
A program may use at most 64 MiB of HBM per device.

v0:
```python
import jax
import jax.numpy as jnp
from jax import lax
from jax.sharding import PartitionSpec as P

SHIFT_MAX = 96
HIST = 5
mixing_share = 0.5
ridge_share = 0.1


def padded_2(block, sides, width, periodic):
    for axis, dim in sides:
        count = lax.axis_size(axis)
        forward = [(i, i + 1) for i in range(count - 1)]
        if periodic:
            forward.append((count - 1, 0))
        backward = [(target, source) for source, target in forward]
        low = lax.ppermute(
            lax.slice_in_dim(block, block.shape[dim] - width, None, axis=dim), axis, forward
        )
        high = lax.ppermute(lax.slice_in_dim(block, 0, width, axis=dim), axis, backward)
        block = jnp.concatenate([low, block, high], axis=dim)
    return block


def emit(padded, margin, length, coupling_row, optical, occupation, shifts):
    lesser = padded[0]
    greater = padded[1]

    def energy_view(source, offset):
        return lax.dynamic_slice_in_dim(source, margin + offset, length, axis=source.ndim - 1)

    sigma_less = coupling_row[:, None] * energy_view(lesser, 0)
    sigma_more = coupling_row[:, None] * energy_view(greater, 0)
    for column in range(2):
        strength = optical[column]
        number = occupation[column]
        offset = shifts[column]
        sigma_less = sigma_less + strength * (
            (number + 1.0) * energy_view(lesser, offset) + number * energy_view(lesser, -offset)
        )
        sigma_more = sigma_more + strength * (
            (number + 1.0) * energy_view(greater, -offset) + number * energy_view(greater, offset)
        )
    return jnp.stack([sigma_less, sigma_more])


def solve_spd(matrix, vector):
    factor = jnp.linalg.cholesky(matrix)
    size_n = matrix.shape[0]
    forward = []
    for column in range(size_n):
        summed = vector[column]
        for earlier in range(column):
            summed = summed - factor[column, earlier] * forward[earlier]
        forward.append(summed / factor[column, column])
    backward = [None] * size_n
    for column in range(size_n - 1, -1, -1):
        summed = forward[column]
        for earlier in range(column + 1, size_n):
            summed = summed - factor[earlier, column] * backward[earlier]
        backward[column] = summed / factor[column, column]
    return jnp.stack(backward)


def mix_weights(products):
    size_n = products.shape[0] - 1
    differ_rows = jnp.eye(size_n, size_n + 1, dtype=jnp.float32) - jnp.eye(
        size_n, size_n + 1, k=1, dtype=jnp.float32
    )
    system = jnp.dot(
        jnp.dot(differ_rows, products, precision=lax.Precision.HIGHEST),
        differ_rows.T,
        precision=lax.Precision.HIGHEST,
    )
    target = jnp.dot(differ_rows, products[:, 0], precision=lax.Precision.HIGHEST)
    ridge = ridge_share * jnp.trace(system) / size_n + 1e-06
    gamma = solve_spd(system + ridge * jnp.eye(size_n, dtype=jnp.float32), target)
    unit = jnp.zeros((size_n + 1,), jnp.float32).at[0].set(1.0)
    return unit - jnp.dot(differ_rows.T, gamma, precision=lax.Precision.HIGHEST)


def per_device(
    greens,
    current,
    past_inputs,
    past_residuals,
    slot_order,
    neighbour,
    momentum_class,
    stencil_weight,
    acoustic_coupling,
    optical_coupling,
    occupation,
    phonon_shift,
):
    group_len = greens.shape[3]
    slice_len = greens.shape[4]
    group_id = lax.axis_index("kgrp")
    total_k = group_len * lax.axis_size("kgrp")
    history = past_residuals.reshape(HIST, -1)
    extended = padded_2(greens, (("kgrp", 3),), group_len, True)
    local_index = (neighbour - group_id * group_len + group_len) % total_k
    smeared = jnp.zeros_like(greens)
    for column in range(5):
        smeared = smeared + stencil_weight[column] * jnp.take(
            extended, local_index[:, column], axis=3
        )
    classes = acoustic_coupling.shape[0]
    coupling_row = jnp.sum(
        jnp.where(
            momentum_class[:, None] == jnp.arange(classes, dtype=jnp.int32)[None, :],
            acoustic_coupling[None, :],
            0.0,
        ),
        axis=1,
    )
    padded = padded_2(smeared, (("energy", 4),), SHIFT_MAX, False)
    sigma_slice = emit(
        padded, SHIFT_MAX, slice_len, coupling_row, optical_coupling, occupation, phonon_shift
    )
    sigma_new = lax.all_to_all(sigma_slice, "energy", split_axis=3, concat_axis=4, tiled=True)
    residual_now = sigma_new - current
    fresh = residual_now.reshape(-1)
    new_local = jnp.concatenate(
        [jnp.sum(fresh * fresh)[None], jnp.dot(history, fresh, precision=lax.Precision.HIGHEST)]
    )
    old_products, new_products = lax.psum(
        (jnp.dot(history, history.T, precision=lax.Precision.HIGHEST), new_local),
        ("kgrp", "energy"),
    )
    entries = float(fresh.shape[0] * lax.axis_size("kgrp") * lax.axis_size("energy"))
    reorder = (slot_order[:, None] == jnp.arange(HIST, dtype=jnp.int32)[None, :]).astype(
        jnp.float32
    )
    old_aged = jnp.dot(
        jnp.dot(reorder, old_products, precision=lax.Precision.HIGHEST),
        reorder.T,
        precision=lax.Precision.HIGHEST,
    )
    new_aged = jnp.dot(reorder, new_products[1:], precision=lax.Precision.HIGHEST)
    top_row = jnp.concatenate([new_products[:1], new_aged])[None, :]
    lower_rows = jnp.concatenate([new_aged[:, None], old_aged], axis=1)
    products = jnp.concatenate([top_row, lower_rows], axis=0) / entries
    weights = mix_weights(products)
    slot_weights = jnp.dot(reorder.T, weights[1:], precision=lax.Precision.HIGHEST)
    mixed = weights[0] * (current + mixing_share * residual_now)
    for column in range(HIST):
        mixed = mixed + slot_weights[column] * (
            past_inputs[column] + mixing_share * past_residuals[column]
        )
    return mixed


def solution(mesh):
    return jax.shard_map(
        per_device,
        mesh=mesh,
        in_specs=(
            P(None, None, None, "kgrp", "energy"),
            P(None, None, None, ("kgrp", "energy"), None),
            P(None, None, None, None, ("kgrp", "energy"), None),
            P(None, None, None, None, ("kgrp", "energy"), None),
            P(),
            P("kgrp", None),
            P("kgrp"),
            P(),
            P(),
            P(),
            P(),
            P(),
        ),
        out_specs=P(None, None, None, ("kgrp", "energy"), None),
        check_vma=False,
    )
```

profile of v0, /device:TPU:1, one launch (start us, length us, event | category | flops | bytes accessed | tf_op | source)
XLA Modules:
  0.0 223.4 jit_solution(8509440534947344868)
XLA Ops:
  0.0 1.2 copy.61
  1.2 3.9 %collective-permute-start = (f32[2,2,2,64,128]{4,2,3,1,0:T(2,128)S(1)}, f32[2,2,2,64,128]{4,2,3,1,0:T(2,128)S(1)}, u32[]{:S(2)}, u32[]{:S(2)}) collective-permute-start(f32[2,2,2,64,128]{4,2,3,1,0:T(2,128)S(1)} %copy.61), channel_id=1, source_target_pairs={{0,32},{32,64},{64,96},{96,128},{128,160},{160,192},{192,224},{224... | collective-permute-start | bytes 786440 | tf_op jit(solution)/shard_map/ppermute | solution.py:19
  5.2 5.6 %collective-permute-start.1 = (f32[2,2,2,64,128]{4,2,3,1,0:T(2,128)S(1)}, f32[2,2,2,64,128]{4,2,3,1,0:T(2,128)S(1)}, u32[]{:S(2)}, u32[]{:S(2)}) collective-permute-start(f32[2,2,2,64,128]{4,2,3,1,0:T(2,128)S(1)} %copy.61), channel_id=1, source_target_pairs={{32,0},{64,32},{96,64},{128,96},{160,128},{192,160},{224,192},{256... | collective-permute-start | bytes 786440 | tf_op jit(solution)/shard_map/ppermute | solution.py:22
  10.8 0.7 add_select_fusion
  11.6 1.4 fusion.50
  12.9 1.3 fusion.49
  19.3 1.5 fusion.51
  20.9 0.2 constant_dynamic-update-slice_fusion.1
  21.2 0.9 gather_fusion.1
  22.1 0.9 gather_fusion.2
  23.0 0.9 gather_fusion.3
  23.9 0.9 gather_fusion.4
  24.8 0.9 gather_fusion
  25.8 3.5 %fusion.11 = f32[2,2,2,64,128]{4,3,2,1,0:T(8,128)S(1)} fusion(f32[64,2,2,2,128]{4,3,2,1,0:T(2,128)S(1)} %gather_fusion.4, f32[64,2,2,2,128]{4,3,2,1,0:T(2,128)S(1)} %gather_fusion.3, f32[64,2,2,2,128]{4,3,2,1,0:T(2,128)S(1)} %gather_fusion.2, f32[64,2,2,2,128]{4,3,2,1,0:T(2,128)S(1)} %gather_fusion.1, f32[64,2,2,2,128]{4,3,2,1,0:T(2,128)S(1)} %gather_fusion, ...), kind=kLoop, calls=%fused_computation.23 | loop fusion | flops 917504 | bytes 1573204 | tf_op jit(solution)/shard_map/add | solution.py:107
  29.3 0.1 fusion.44
  29.5 4.5 %collective-permute-start.2 = (f32[2,2,2,64,96]{4,3,2,1,0:T(8,128)S(1)}, f32[2,2,2,64,96]{4,3,2,1,0:T(8,128)S(1)}, u32[]{:S(2)}, u32[]{:S(2)}) collective-permute-start(f32[2,2,2,64,96]{4,3,2,1,0:T(8,128)S(1)} %get-tuple-element.36), channel_id=1, source_target_pairs={{0,1},{1,2},{2,3},{3,4},{4,5},{5,6},{6,7},{7,8},{8,9},{9,10},{10,1... | collective-permute-start | bytes 589832 | tf_op jit(solution)/shard_map/ppermute | solution.py:19
  34.0 5.2 %collective-permute-start.3 = (f32[2,2,2,64,96]{4,3,2,1,0:T(8,128)S(1)}, f32[2,2,2,64,96]{4,3,2,1,0:T(8,128)S(1)}, u32[]{:S(2)}, u32[]{:S(2)}) collective-permute-start(f32[2,2,2,64,96]{4,3,2,1,0:T(8,128)S(1)} %get-tuple-element.37), channel_id=1, source_target_pairs={{1,0},{2,1},{3,2},{4,3},{5,4},{6,5},{7,6},{8,7},{9,8},{10,9},{11,1... | collective-permute-start | bytes 589832 | tf_op jit(solution)/shard_map/ppermute | solution.py:22
  39.2 0.6 fusion.48
  39.9 1.8 collective-permute-done.3
  41.7 0.3 pad_maximum_fusion
  42.0 0.2 fusion.43
  42.2 3.0 %fusion.21 = (f32[1,2,2,64,128]{4,3,2,1,0:T(8,128)S(1)}, f32[1,2,2,64,128]{4,3,2,1,0:T(8,128)S(1)}) fusion(f32[2,2,64,320]{3,2,1,0:T(8,128)S(1)} %get-tuple-element.31, f32[1,2,2,64,320]{4,3,2,1,0:T(8,128)S(1)} %get-tuple-element.30, s32[]{:T(128)S(6)} %select_n.48, s32[]{:T(128)S(6)} %select_n.47, s32[]{:T(128)S(6)} %select_n.46, s32[]{:T(128)S(6)} %select_n.45, ...), kind=kLoop, calls=%fused_computation.45 | loop fusion | flops 720896 | bytes 1573160 | tf_op jit(solution)/shard_map/stack | solution.py:46
  45.2 0.9 copy.69
  46.1 15.2 %all-to-all-start = ((f32[2,2,2,64,128]{4,2,1,0,3:T(2,128)}), f32[2,2,2,64,128]{4,2,1,0,3:T(2,128)S(1)}, u32[]{:S(2)}, u32[]{:S(2)}) async-start(f32[2,2,2,64,128]{4,2,1,0,3:T(2,128)} %copy.69), calls=%async_computation | async-start | bytes 524288 | tf_op jit(solution)/shard_map/all_to_all | solution.py:123
  61.4 5.2 %fusion.4 = f32[5,5]{1,0:T(8,128)S(1)} fusion(f32[5,2,2,2,2,4096]{5,4,3,2,1,0:T(2,128)S(1)} %copy-done), kind=kOutput, calls=%fused_computation.9 | convolution fusion | flops 19660800 | bytes 1310820 | tf_op jit(solution)/shard_map/dot_general | solution.py:130
  66.5 16.8 %all-to-all-done = f32[2,2,2,64,128]{4,2,1,0,3:T(2,128)S(1)} async-done(((f32[2,2,2,64,128]{4,2,1,0,3:T(2,128)}), f32[2,2,2,64,128]{4,2,1,0,3:T(2,128)S(1)}, u32[]{:S(2)}, u32[]{:S(2)}) %all-to-all-start) | async-done | bytes 262176 | tf_op jit(solution)/shard_map/all_to_all | solution.py:123
  83.4 0.1 all_to_all.16
  83.6 0.9 multiply_reduce_fusion
  84.5 4.8 %fusion.7 = f32[5]{0:T(128)S(1)} fusion(f32[5,2,2,2,2,4096]{5,4,3,2,1,0:T(2,128)S(1)} %copy-done, f32[2,2,2,2,4096,1]{4,3,2,1,0,5:T(2,128)S(1)} %get-tuple-element.35), kind=kOutput, calls=%fused_computation.12 | convolution fusion | flops 3932160 | bytes 1572884 | tf_op jit(solution)/shard_map/dot_general | solution.py:127
  89.2 0.7 pad_maximum_fusion.2
  90.0 99.0 %all-reduce = (f32[5,5]{1,0:T(8,128)S(1)}, f32[6]{0:T(128)S(1)}) all-reduce(f32[5,5]{1,0:T(8,128)S(1)} %fusion.4, f32[6]{0:T(128)S(1)} %pad_maximum_fusion.2), channel_id=1, replica_groups=mesh['kgrp'=16,'energy'=32] {'kgrp','energy'}, use_global_device_ids=true, to_apply=%region_3.5 | all-reduce | flops 31 | bytes 248 | tf_op jit(solution)/shard_map/psum | solution.py:129
  189.0 0.2 fusion.27
  189.2 0.1 maximum_bitcast_fusion
  189.3 0.1 copy.73
  189.4 0.2 fusion.26
  189.6 0.2 fusion.25
  189.9 0.2 fusion.29
  190.1 0.2 convolution_bitcast_fusion.1
  190.3 0.8 select_reduce_fusion.1
  191.8 0.4 cholesky.21
  192.3 0.6 compare_reduce_fusion
  193.0 0.6 select_select_fusion
  193.6 0.7 fusion.45
  194.3 0.7 fusion.47
  217.4 0.1 fusion.10
  217.6 0.2 convolution_bitcast_fusion.2
  217.7 0.7 fusion.46
  218.4 5.0 %bitcast_add_fusion = f32[2,2,2,2,4096]{4,3,2,1,0:T(2,128)} fusion(f32[5,2,2,2,2,4096]{5,4,3,2,1,0:T(2,128)S(1)} %copy-done, f32[5,2,2,2,2,4096]{5,4,3,2,1,0:T(2,128)S(1)} %copy-done.1, f32[2,2,2,2,4096]{4,3,2,1,0:T(2,128)S(1)} %copy-done.3, f32[]{:T(128)} %bitcast.88, f32[]{:T(128)} %bitcast.86, f32[]{:T(128)} %bitcast.84, f32[]{:T(128)} %bitcast.82, ...), kind=kLoop, calls=%fused_computation.17 | loop fusion | flops 1572864 | bytes 3407896 | tf_op jit(solution)/shard_map/add | solution.py:150
  (36 shorter events, 0.6 us)
Async XLA Ops:
  0.0 20.9 %copy-start.2 = (f32[2,2,2,64,128]{4,3,2,1,0:T(8,128)S(1)}, f32[2,2,2,64,128]{4,3,2,1,0:T(8,128)}, u32[]{:S(2)}) copy-start(f32[2,2,2,64,128]{4,3,2,1,0:T(8,128)} %param.16) | copy-start | bytes 786436
  1.2 19.6 %collective-permute-start = (f32[2,2,2,64,128]{4,2,3,1,0:T(2,128)S(1)}, f32[2,2,2,64,128]{4,2,3,1,0:T(2,128)S(1)}, u32[]{:S(2)}, u32[]{:S(2)}) collective-permute-start(f32[2,2,2,64,128]{4,2,3,1,0:T(2,128)S(1)} %copy.61), channel_id=1, source_target_pairs={{0,32},{32,64},{64,96},{96,128},{128,160},{160,192},{192,224},{224... | collective-permute-start | bytes 786440 | tf_op jit(solution)/shard_map/ppermute | solution.py:19
  5.2 15.9 %collective-permute-start.1 = (f32[2,2,2,64,128]{4,2,3,1,0:T(2,128)S(1)}, f32[2,2,2,64,128]{4,2,3,1,0:T(2,128)S(1)}, u32[]{:S(2)}, u32[]{:S(2)}) collective-permute-start(f32[2,2,2,64,128]{4,2,3,1,0:T(2,128)S(1)} %copy.61), channel_id=1, source_target_pairs={{32,0},{64,32},{96,64},{128,96},{160,128},{192,160},{224,192},{256... | collective-permute-start | bytes 786440 | tf_op jit(solution)/shard_map/ppermute | solution.py:22
  25.7 13.4 %copy-start.4 = (f32[2]{0:T(128)S(1)}, f32[2]{0:T(128)}, u32[]{:S(2)}) copy-start(f32[2]{0:T(128)} %param.25) | copy-start | bytes 28
  25.8 14.0 %copy-start.5 = (f32[4]{0:T(128)S(1)}, f32[4]{0:T(128)}, u32[]{:S(2)}) copy-start(f32[4]{0:T(128)} %param.24) | copy-start | bytes 52
  25.8 14.0 %copy-start.6 = (s32[64]{0:T(128)S(1)}, s32[64]{0:T(128)}, u32[]{:S(2)}) copy-start(s32[64]{0:T(128)} %param.22) | copy-start | bytes 772
  29.5 10.4 %collective-permute-start.2 = (f32[2,2,2,64,96]{4,3,2,1,0:T(8,128)S(1)}, f32[2,2,2,64,96]{4,3,2,1,0:T(8,128)S(1)}, u32[]{:S(2)}, u32[]{:S(2)}) collective-permute-start(f32[2,2,2,64,96]{4,3,2,1,0:T(8,128)S(1)} %get-tuple-element.36), channel_id=1, source_target_pairs={{0,1},{1,2},{2,3},{3,4},{4,5},{5,6},{6,7},{7,8},{8,9},{9,10},{10,1... | collective-permute-start | bytes 589832 | tf_op jit(solution)/shard_map/ppermute | solution.py:19
  34.0 7.7 %collective-permute-start.3 = (f32[2,2,2,64,96]{4,3,2,1,0:T(8,128)S(1)}, f32[2,2,2,64,96]{4,3,2,1,0:T(8,128)S(1)}, u32[]{:S(2)}, u32[]{:S(2)}) collective-permute-start(f32[2,2,2,64,96]{4,3,2,1,0:T(8,128)S(1)} %get-tuple-element.37), channel_id=1, source_target_pairs={{1,0},{2,1},{3,2},{4,3},{5,4},{6,5},{7,6},{8,7},{9,8},{10,9},{11,1... | collective-permute-start | bytes 589832 | tf_op jit(solution)/shard_map/ppermute | solution.py:22
  42.2 19.2 %copy-start = (f32[5,2,2,2,2,4096]{5,4,3,2,1,0:T(2,128)S(1)}, f32[5,2,2,2,2,4096]{5,4,3,2,1,0:T(2,128)}, u32[]{:S(2)}) copy-start(f32[5,2,2,2,2,4096]{5,4,3,2,1,0:T(2,128)} %param.19) | copy-start | bytes 3932164
  46.1 37.2 %all-to-all-start = ((f32[2,2,2,64,128]{4,2,1,0,3:T(2,128)}), f32[2,2,2,64,128]{4,2,1,0,3:T(2,128)S(1)}, u32[]{:S(2)}, u32[]{:S(2)}) async-start(f32[2,2,2,64,128]{4,2,1,0,3:T(2,128)} %copy.69), calls=%async_computation | async-start | bytes 524288 | tf_op jit(solution)/shard_map/all_to_all | solution.py:123
  61.4 22.2 %copy-start.3 = (f32[2,2,2,2,4096]{4,3,2,1,0:T(2,128)S(1)}, f32[2,2,2,2,4096]{4,3,2,1,0:T(2,128)}, u32[]{:S(2)}) copy-start(f32[2,2,2,2,4096]{4,3,2,1,0:T(2,128)} %param.17) | copy-start | bytes 786436
  84.5 104.5 %copy-start.7 = (s32[5]{0:T(128)S(1)}, s32[5]{0:T(128)}, u32[]{:S(2)}) copy-start(s32[5]{0:T(128)} %param.20) | copy-start | bytes 64
  84.5 132.9 %copy-start.8 = (f32[6]{0:T(128)S(1)}, f32[6]{0:T(128)}, u32[]{:S(2)}) copy-start(f32[6]{0:T(128)} %constant.127.clone.1) | copy-start | bytes 76
  84.5 133.9 %copy-start.1 = (f32[5,2,2,2,2,4096]{5,4,3,2,1,0:T(2,128)S(1)}, f32[5,2,2,2,2,4096]{5,4,3,2,1,0:T(2,128)}, u32[]{:S(2)}) copy-start(f32[5,2,2,2,2,4096]{5,4,3,2,1,0:T(2,128)} %param.18) | copy-start | bytes 3932164
where the time goes:
time: 224 us; the launch traced here: 223 us
  blocking collectives  99 us (44%)
  starting transfers between devices  34.5 us (15%)
  between operations  28.3 us (13%)
  waiting for transfers between devices  18.6 us (8%)
  other arithmetic  16.3 us (7%)
  local copies, waits for them, and re-layouts  14.7 us (7%)
  matrix products  12 us (5%)
    psum x1, blocking collectives, per_device(): lax.psum((jnp.dot(history, history.T, precision=lax.Precision.HIGHEST), n...  99 us
    all_to_all x1, waiting for transfers between devices, per_device(): lax.all_to_all(sigma_slice, 'energy', split_axis=3, concat_axis=4, tiled=...  16.8 us
    all_to_all x1, starting transfers between devices, per_device(): lax.all_to_all(sigma_slice, 'energy', split_axis=3, concat_axis=4, tiled=...  15.2 us
    ppermute x2, starting transfers between devices, padded_2(): lax.ppermute(lax.slice_in_dim(block, 0, width, axis=dim), axis, backward)  10.8 us
    ppermute x2, starting transfers between devices, padded_2(): lax.ppermute(lax.slice_in_dim(block, block.shape[dim] - width, None, axis...  8.46 us
    dot_general x1, matrix products, per_device(): jnp.dot(history, history.T, precision=lax.Precision.HIGHEST)  5.16 us
    add x1, other arithmetic, per_device(): mixed + slot_weights[column] * (past_inputs[column] + mixing_share * past...  4.95 us
    dot_general x1, matrix products, per_device(): jnp.dot(history, fresh, precision=lax.Precision.HIGHEST)  4.76 us
  transfers between devices with their start and end apart: 5, of which 2 were waited for; matrix products, arithmetic and copies ran while one was open for 5% of the time, Pallas kernels for 0%

commit v1 on v0

--- a/solution.py
+++ b/solution.py
@@ -126,9 +126,12 @@
     new_local = jnp.concatenate(
         [jnp.sum(fresh * fresh)[None], jnp.dot(history, fresh, precision=lax.Precision.HIGHEST)]
     )
-    old_products, new_products = lax.psum(
-        (jnp.dot(history, history.T, precision=lax.Precision.HIGHEST), new_local),
-        ("kgrp", "energy"),
+    old_products, new_products = jax.lax.psum(
+        jax.lax.psum(
+            (jnp.dot(history, history.T, precision=lax.Precision.HIGHEST), new_local),
+            axis_name="kgrp",
+        ),
+        axis_name="energy",
     )
     entries = float(fresh.shape[0] * lax.axis_size("kgrp") * lax.axis_size("energy"))
     reorder = (slot_order[:, None] == jnp.arange(HIST, dtype=jnp.int32)[None, :]).astype(

time: 224 us -> 210 us (0.938)
  blocking collectives: 99 us -> 84.9 us
    psum x1 -> x2, blocking collectives: 99 us -> 84.9 us  [the longest x1 54.4 us: per_device(): jax.lax.psum(jax.lax.psum((jnp.dot(history, history.T, precision=lax.Prec...]
where the time goes in v1:
time: 210 us; the launch traced here: 209 us
  blocking collectives  84.9 us (40%)
  starting transfers between devices  34.5 us (16%)
  between operations  28.2 us (13%)
  waiting for transfers between devices  18.6 us (9%)
  other arithmetic  16.3 us (8%)
  local copies, waits for them, and re-layouts  14.6 us (7%)
  matrix products  12 us (6%)
    psum x1, blocking collectives, per_device(): jax.lax.psum(jax.lax.psum((jnp.dot(history, history.T, precision=lax.Prec...  54.4 us
    psum x1, blocking collectives, per_device(): jax.lax.psum((jnp.dot(history, history.T, precision=lax.Precision.HIGHEST...  30.6 us
    all_to_all x1, waiting for transfers between devices, per_device(): lax.all_to_all(sigma_slice, 'energy', split_axis=3, concat_axis=4, tiled=...  16.8 us
    all_to_all x1, starting transfers between devices, per_device(): lax.all_to_all(sigma_slice, 'energy', split_axis=3, concat_axis=4, tiled=...  15.2 us
    ppermute x2, starting transfers between devices, padded_2(): lax.ppermute(lax.slice_in_dim(block, 0, width, axis=dim), axis, backward)  10.8 us
    ppermute x2, starting transfers between devices, padded_2(): lax.ppermute(lax.slice_in_dim(block, block.shape[dim] - width, None, axis...  8.46 us
    dot_general x1, matrix products, per_device(): jnp.dot(history, history.T, precision=lax.Precision.HIGHEST)  5.16 us
    add x1, other arithmetic, per_device(): mixed + slot_weights[column] * (past_inputs[column] + mixing_share * past...  5.03 us
  transfers between devices with their start and end apart: 5, of which 2 were waited for; matrix products, arithmetic and copies ran while one was open for 5% of the time, Pallas kernels for 0%

profile of v1, /device:TPU:1, one launch (start us, length us, event | category | flops | bytes accessed | tf_op | source)
XLA Modules:
  0.0 209.1 jit_solution(3127257217633788889)
XLA Ops:
  0.0 1.2 copy.61
  1.2 3.9 %collective-permute-start = (f32[2,2,2,64,128]{4,2,3,1,0:T(2,128)S(1)}, f32[2,2,2,64,128]{4,2,3,1,0:T(2,128)S(1)}, u32[]{:S(2)}, u32[]{:S(2)}) collective-permute-start(f32[2,2,2,64,128]{4,2,3,1,0:T(2,128)S(1)} %copy.61), channel_id=1, source_target_pairs={{0,32},{32,64},{64,96},{96,128},{128,160},{160,192},{192,224},{224... | collective-permute-start | bytes 786440 | tf_op jit(solution)/shard_map/ppermute | solution.py:19
  5.2 5.6 %collective-permute-start.1 = (f32[2,2,2,64,128]{4,2,3,1,0:T(2,128)S(1)}, f32[2,2,2,64,128]{4,2,3,1,0:T(2,128)S(1)}, u32[]{:S(2)}, u32[]{:S(2)}) collective-permute-start(f32[2,2,2,64,128]{4,2,3,1,0:T(2,128)S(1)} %copy.61), channel_id=1, source_target_pairs={{32,0},{64,32},{96,64},{128,96},{160,128},{192,160},{224,192},{256... | collective-permute-start | bytes 786440 | tf_op jit(solution)/shard_map/ppermute | solution.py:22
  10.8 0.7 add_select_fusion
  11.6 1.3 fusion.50
  12.9 1.3 fusion.49
  19.1 1.5 fusion.51
  20.7 0.2 constant_dynamic-update-slice_fusion.1
  20.9 0.9 gather_fusion.1
  21.9 0.9 gather_fusion.2
  22.8 0.9 gather_fusion.3
  23.7 0.9 gather_fusion.4
  24.6 0.9 gather_fusion
  25.6 3.5 %fusion.11 = f32[2,2,2,64,128]{4,3,2,1,0:T(8,128)S(1)} fusion(f32[64,2,2,2,128]{4,3,2,1,0:T(2,128)S(1)} %gather_fusion.4, f32[64,2,2,2,128]{4,3,2,1,0:T(2,128)S(1)} %gather_fusion.3, f32[64,2,2,2,128]{4,3,2,1,0:T(2,128)S(1)} %gather_fusion.2, f32[64,2,2,2,128]{4,3,2,1,0:T(2,128)S(1)} %gather_fusion.1, f32[64,2,2,2,128]{4,3,2,1,0:T(2,128)S(1)} %gather_fusion, ...), kind=kLoop, calls=%fused_computation.23 | loop fusion | flops 917504 | bytes 1573204 | tf_op jit(solution)/shard_map/add | solution.py:107
  29.1 0.1 fusion.44
  29.2 4.5 %collective-permute-start.2 = (f32[2,2,2,64,96]{4,3,2,1,0:T(8,128)S(1)}, f32[2,2,2,64,96]{4,3,2,1,0:T(8,128)S(1)}, u32[]{:S(2)}, u32[]{:S(2)}) collective-permute-start(f32[2,2,2,64,96]{4,3,2,1,0:T(8,128)S(1)} %get-tuple-element.38), channel_id=1, source_target_pairs={{0,1},{1,2},{2,3},{3,4},{4,5},{5,6},{6,7},{7,8},{8,9},{9,10},{10,1... | collective-permute-start | bytes 589832 | tf_op jit(solution)/shard_map/ppermute | solution.py:19
  33.7 5.2 %collective-permute-start.3 = (f32[2,2,2,64,96]{4,3,2,1,0:T(8,128)S(1)}, f32[2,2,2,64,96]{4,3,2,1,0:T(8,128)S(1)}, u32[]{:S(2)}, u32[]{:S(2)}) collective-permute-start(f32[2,2,2,64,96]{4,3,2,1,0:T(8,128)S(1)} %get-tuple-element.39), channel_id=1, source_target_pairs={{1,0},{2,1},{3,2},{4,3},{5,4},{6,5},{7,6},{8,7},{9,8},{10,9},{11,1... | collective-permute-start | bytes 589832 | tf_op jit(solution)/shard_map/ppermute | solution.py:22
  38.9 0.6 fusion.48
  39.6 1.8 collective-permute-done.3
  41.4 0.3 pad_maximum_fusion
  41.8 0.2 fusion.43
  41.9 3.0 %fusion.21 = (f32[1,2,2,64,128]{4,3,2,1,0:T(8,128)S(1)}, f32[1,2,2,64,128]{4,3,2,1,0:T(8,128)S(1)}) fusion(f32[2,2,64,320]{3,2,1,0:T(8,128)S(1)} %get-tuple-element.33, f32[1,2,2,64,320]{4,3,2,1,0:T(8,128)S(1)} %get-tuple-element.32, s32[]{:T(128)S(6)} %select_n.48, s32[]{:T(128)S(6)} %select_n.47, s32[]{:T(128)S(6)} %select_n.46, s32[]{:T(128)S(6)} %select_n.45, ...), kind=kLoop, calls=%fused_computation.45 | loop fusion | flops 720896 | bytes 1573160 | tf_op jit(solution)/shard_map/stack | solution.py:46
  45.0 0.9 copy.69
  45.9 15.2 %all-to-all-start = ((f32[2,2,2,64,128]{4,2,1,0,3:T(2,128)}), f32[2,2,2,64,128]{4,2,1,0,3:T(2,128)S(1)}, u32[]{:S(2)}, u32[]{:S(2)}) async-start(f32[2,2,2,64,128]{4,2,1,0,3:T(2,128)} %copy.69), calls=%async_computation | async-start | bytes 524288 | tf_op jit(solution)/shard_map/all_to_all | solution.py:123
  61.2 5.2 %fusion.4 = f32[5,5]{1,0:T(8,128)S(1)} fusion(f32[5,2,2,2,2,4096]{5,4,3,2,1,0:T(2,128)S(1)} %copy-done), kind=kOutput, calls=%fused_computation.9 | convolution fusion | flops 19660800 | bytes 1310820 | tf_op jit(solution)/shard_map/dot_general | solution.py:131
  66.3 16.8 %all-to-all-done = f32[2,2,2,64,128]{4,2,1,0,3:T(2,128)S(1)} async-done(((f32[2,2,2,64,128]{4,2,1,0,3:T(2,128)}), f32[2,2,2,64,128]{4,2,1,0,3:T(2,128)S(1)}, u32[]{:S(2)}, u32[]{:S(2)}) %all-to-all-start) | async-done | bytes 262176 | tf_op jit(solution)/shard_map/all_to_all | solution.py:123
  83.2 0.1 all_to_all.16
  83.4 0.9 multiply_reduce_fusion
  84.2 4.8 %fusion.7 = f32[5]{0:T(128)S(1)} fusion(f32[5,2,2,2,2,4096]{5,4,3,2,1,0:T(2,128)S(1)} %copy-done, f32[2,2,2,2,4096,1]{4,3,2,1,0,5:T(2,128)S(1)} %get-tuple-element.37), kind=kOutput, calls=%fused_computation.12 | convolution fusion | flops 3932160 | bytes 1572884 | tf_op jit(solution)/shard_map/dot_general | solution.py:127
  89.0 0.7 pad_maximum_fusion.2
  89.7 30.6 %all-reduce.1 = (f32[5,5]{1,0:T(8,128)S(1)}, f32[6]{0:T(128)S(1)}) all-reduce(f32[5,5]{1,0:T(8,128)S(1)} %fusion.4, f32[6]{0:T(128)S(1)} %pad_maximum_fusion.2), channel_id=1, replica_groups=mesh['kgrp'=16,'energy'=32] {'kgrp'}, use_global_device_ids=true, to_apply=%region_4.6 | all-reduce | flops 31 | bytes 248 | tf_op jit(solution)/shard_map/psum | solution.py:130
  120.3 54.4 %all-reduce = (f32[5,5]{1,0:T(8,128)S(1)}, f32[6]{0:T(128)S(1)}) all-reduce(f32[5,5]{1,0:T(8,128)S(1)} %get-tuple-element.20, f32[6]{0:T(128)S(1)} %get-tuple-element.21), channel_id=1, replica_groups=mesh['kgrp'=16,'energy'=32] {'energy'}, use_global_device_ids=true, to_apply=%region_5.7 | all-reduce | flops 31 | bytes 248 | tf_op jit(solution)/shard_map/psum | solution.py:129
  174.7 0.2 fusion.27
  174.9 0.1 maximum_bitcast_fusion
  175.1 0.2 fusion.26
  175.3 0.2 fusion.25
  175.6 0.2 fusion.29
  175.8 0.2 convolution_bitcast_fusion.1
  176.0 0.8 select_reduce_fusion.1
  177.5 0.4 cholesky.21
  178.0 0.6 compare_reduce_fusion
  178.7 0.6 select_select_fusion
  179.3 0.7 fusion.45
  180.0 0.7 fusion.47
  203.1 0.1 fusion.10
  203.2 0.2 convolution_bitcast_fusion.2
  203.4 0.7 fusion.46
  204.1 5.0 %bitcast_add_fusion = f32[2,2,2,2,4096]{4,3,2,1,0:T(2,128)} fusion(f32[5,2,2,2,2,4096]{5,4,3,2,1,0:T(2,128)S(1)} %copy-done, f32[5,2,2,2,2,4096]{5,4,3,2,1,0:T(2,128)S(1)} %copy-done.1, f32[2,2,2,2,4096]{4,3,2,1,0:T(2,128)S(1)} %copy-done.3, f32[]{:T(128)} %bitcast.88, f32[]{:T(128)} %bitcast.86, f32[]{:T(128)} %bitcast.84, f32[]{:T(128)} %bitcast.82, ...), kind=kLoop, calls=%fused_computation.17 | loop fusion | flops 1572864 | bytes 3407896 | tf_op jit(solution)/shard_map/add | solution.py:153
  (37 shorter events, 0.7 us)
Async XLA Ops:
  0.0 20.7 %copy-start.2 = (f32[2,2,2,64,128]{4,3,2,1,0:T(8,128)S(1)}, f32[2,2,2,64,128]{4,3,2,1,0:T(8,128)}, u32[]{:S(2)}) copy-start(f32[2,2,2,64,128]{4,3,2,1,0:T(8,128)} %param.16) | copy-start | bytes 786436
  1.2 19.4 %collective-permute-start = (f32[2,2,2,64,128]{4,2,3,1,0:T(2,128)S(1)}, f32[2,2,2,64,128]{4,2,3,1,0:T(2,128)S(1)}, u32[]{:S(2)}, u32[]{:S(2)}) collective-permute-start(f32[2,2,2,64,128]{4,2,3,1,0:T(2,128)S(1)} %copy.61), channel_id=1, source_target_pairs={{0,32},{32,64},{64,96},{96,128},{128,160},{160,192},{192,224},{224... | collective-permute-start | bytes 786440 | tf_op jit(solution)/shard_map/ppermute | solution.py:19
  5.2 15.7 %collective-permute-start.1 = (f32[2,2,2,64,128]{4,2,3,1,0:T(2,128)S(1)}, f32[2,2,2,64,128]{4,2,3,1,0:T(2,128)S(1)}, u32[]{:S(2)}, u32[]{:S(2)}) collective-permute-start(f32[2,2,2,64,128]{4,2,3,1,0:T(2,128)S(1)} %copy.61), channel_id=1, source_target_pairs={{32,0},{64,32},{96,64},{128,96},{160,128},{192,160},{224,192},{256... | collective-permute-start | bytes 786440 | tf_op jit(solution)/shard_map/ppermute | solution.py:22
  25.5 13.4 %copy-start.4 = (f32[2]{0:T(128)S(1)}, f32[2]{0:T(128)}, u32[]{:S(2)}) copy-start(f32[2]{0:T(128)} %param.25) | copy-start | bytes 28
  25.6 13.9 %copy-start.5 = (f32[4]{0:T(128)S(1)}, f32[4]{0:T(128)}, u32[]{:S(2)}) copy-start(f32[4]{0:T(128)} %param.24) | copy-start | bytes 52
  25.6 13.9 %copy-start.6 = (s32[64]{0:T(128)S(1)}, s32[64]{0:T(128)}, u32[]{:S(2)}) copy-start(s32[64]{0:T(128)} %param.22) | copy-start | bytes 772
  29.2 10.4 %collective-permute-start.2 = (f32[2,2,2,64,96]{4,3,2,1,0:T(8,128)S(1)}, f32[2,2,2,64,96]{4,3,2,1,0:T(8,128)S(1)}, u32[]{:S(2)}, u32[]{:S(2)}) collective-permute-start(f32[2,2,2,64,96]{4,3,2,1,0:T(8,128)S(1)} %get-tuple-element.38), channel_id=1, source_target_pairs={{0,1},{1,2},{2,3},{3,4},{4,5},{5,6},{6,7},{7,8},{8,9},{9,10},{10,1... | collective-permute-start | bytes 589832 | tf_op jit(solution)/shard_map/ppermute | solution.py:19
  33.7 7.7 %collective-permute-start.3 = (f32[2,2,2,64,96]{4,3,2,1,0:T(8,128)S(1)}, f32[2,2,2,64,96]{4,3,2,1,0:T(8,128)S(1)}, u32[]{:S(2)}, u32[]{:S(2)}) collective-permute-start(f32[2,2,2,64,96]{4,3,2,1,0:T(8,128)S(1)} %get-tuple-element.39), channel_id=1, source_target_pairs={{1,0},{2,1},{3,2},{4,3},{5,4},{6,5},{7,6},{8,7},{9,8},{10,9},{11,1... | collective-permute-start | bytes 589832 | tf_op jit(solution)/shard_map/ppermute | solution.py:22
  41.9 19.2 %copy-start = (f32[5,2,2,2,2,4096]{5,4,3,2,1,0:T(2,128)S(1)}, f32[5,2,2,2,2,4096]{5,4,3,2,1,0:T(2,128)}, u32[]{:S(2)}) copy-start(f32[5,2,2,2,2,4096]{5,4,3,2,1,0:T(2,128)} %param.19) | copy-start | bytes 3932164
  45.9 37.2 %all-to-all-start = ((f32[2,2,2,64,128]{4,2,1,0,3:T(2,128)}), f32[2,2,2,64,128]{4,2,1,0,3:T(2,128)S(1)}, u32[]{:S(2)}, u32[]{:S(2)}) async-start(f32[2,2,2,64,128]{4,2,1,0,3:T(2,128)} %copy.69), calls=%async_computation | async-start | bytes 524288 | tf_op jit(solution)/shard_map/all_to_all | solution.py:123
  61.1 22.2 %copy-start.3 = (f32[2,2,2,2,4096]{4,3,2,1,0:T(2,128)S(1)}, f32[2,2,2,2,4096]{4,3,2,1,0:T(2,128)}, u32[]{:S(2)}) copy-start(f32[2,2,2,2,4096]{4,3,2,1,0:T(2,128)} %param.17) | copy-start | bytes 786436
  84.2 90.4 %copy-start.7 = (s32[5]{0:T(128)S(1)}, s32[5]{0:T(128)}, u32[]{:S(2)}) copy-start(s32[5]{0:T(128)} %param.20) | copy-start | bytes 64
  84.2 118.8 %copy-start.8 = (f32[6]{0:T(128)S(1)}, f32[6]{0:T(128)}, u32[]{:S(2)}) copy-start(f32[6]{0:T(128)} %constant.127.clone.1) | copy-start | bytes 76
  84.2 119.8 %copy-start.1 = (f32[5,2,2,2,2,4096]{5,4,3,2,1,0:T(2,128)S(1)}, f32[5,2,2,2,2,4096]{5,4,3,2,1,0:T(2,128)}, u32[]{:S(2)}) copy-start(f32[5,2,2,2,2,4096]{5,4,3,2,1,0:T(2,128)} %param.18) | copy-start | bytes 3932164
